TPU v7x, 256 devices: a whole 4x4x8 slice. The times are simulated.
256 devices in a mesh: freq: 32 (over x, y, core), node: 8 (over z).
Axes of the slice: x: 4, y: 4, z: 8, core: 2. Of those that a mesh axis runs over, the one named last changes fastest.
Arguments:
- pressure: bfloat16 [2, 128, 4, 65536], P(None, 'freq', None, 'node'), may hold values from -6 to 6
- spectrum_amp: float32 [4, 128], replicated, may hold values from 0.03 to 0.3
- phase_code: int32 [4, 128], replicated, may hold values from 0 to 4095
- panel_tile: int32 [32, 8, 256, 1], P('freq'), may hold values from 0 to 255; in each aligned block of 2048 rows (0 to 2047, 2048 to 4095, ..., all dimensions but the last counted through in order) at most 12 rows name the same one
- patch_weight: bfloat16 [32, 8, 256, 128], P('freq'), may hold values from 0 to 0.099609375
Outputs:
- node_loads: bfloat16 [4, 4096, 32768], P(None, 'node', 'freq')
Inputs may be any that keep to these rules, and one draw needn't show every extreme that they name: Within each block panel_tile[g] (2048 panels), no patch is named by more than 12 panels, a bound that some block reaches; every patch is named somewhere.
All inputs are finite; a program needn't handle non-finite values.
Results may differ from a plain program's by a relative error of at most 0.0062.
Values may be sent and summed in bfloat16 or wider, within the bound.
No kernel may reach another device: no remote copies, remote signals or barrier semaphores. Data moves between devices by JAX's collectives and lax.ppermute only.
A program may use at most 128 MiB of HBM per device.

v0:
```python
import math
import jax
import jax.numpy as jnp
from jax import lax
from jax.sharding import PartitionSpec as P

F = 128
TSTEPS = 4096
BIN_STEP = 15
PHASE_LEVELS = 4096
TILE_DEV = 8


def scale_spectra(pressure, spectrum_amp, phase_code):
    phase_angle = phase_code.astype(jnp.float32) * (2.0 * math.pi / PHASE_LEVELS)
    amplitude = spectrum_amp.T[:, :, None]
    cosine = jnp.cos(phase_angle).T[:, :, None]
    sine_part = jnp.sin(phase_angle).T[:, :, None]
    real_part = pressure[0].astype(jnp.float32)
    imag_part = pressure[1].astype(jnp.float32)
    scaled_re = amplitude * (real_part * cosine - imag_part * sine_part)
    scaled_im = amplitude * (real_part * sine_part + imag_part * cosine)
    return jnp.stack([scaled_re, scaled_im]).astype(jnp.bfloat16)


def basis_table(step_count):
    freq_bin = 1 + BIN_STEP * jnp.arange(F, dtype=jnp.int32)
    step_ids = jnp.arange(step_count, dtype=jnp.int32)
    turn_count = freq_bin[:, None] * step_ids[None, :] % TSTEPS
    turn_angle = turn_count.astype(jnp.float32) * (2.0 * math.pi / TSTEPS)
    return jnp.concatenate([jnp.cos(turn_angle), -jnp.sin(turn_angle)], axis=0).astype(jnp.bfloat16)


def slot_members(tile_ids, tile_count, capacity):
    row_count = tile_ids.shape[0]
    onehot = (tile_ids[:, None] == jnp.arange(tile_count, dtype=jnp.int32)[None, :]).astype(
        jnp.int32
    )
    slot_rank = jnp.sum((jnp.cumsum(onehot, axis=0) - onehot) * onehot, axis=1)
    slot_index = tile_ids * capacity + slot_rank
    empty = jnp.full((tile_count * capacity,), row_count, jnp.int32)
    return empty.at[slot_index].set(jnp.arange(row_count, dtype=jnp.int32))


def shards(pressure, spectrum_amp, phase_code, panel_tile, patch_weight):
    regrouped = lax.all_to_all(pressure, "freq", split_axis=3, concat_axis=1, tiled=True)
    scaled = scale_spectra(regrouped, spectrum_amp, phase_code)
    freq_count = scaled.shape[1]
    headings = scaled.shape[2]
    panels = scaled.shape[3]
    owners = lax.axis_size("freq")
    windows = lax.axis_size("node")
    window_len = TSTEPS // windows
    tile_count = owners * TILE_DEV
    capacity = max(2, 3 * windows * panels // (2 * TILE_DEV * owners))
    tile_ids = panel_tile.reshape(-1)
    weights = patch_weight.reshape(-1, 128)
    members = slot_members(tile_ids, tile_count, capacity)
    sent_weight = jnp.take(weights, members, axis=0, mode="fill", fill_value=0)
    sent_weight = sent_weight.reshape(1, owners, TILE_DEV, capacity, 128)
    wave_basis = basis_table(TSTEPS)
    series = jnp.einsum(
        "khp,kt->hpt",
        scaled.reshape(2 * freq_count, headings, panels),
        wave_basis,
        preferred_element_type=jnp.float32,
    ).astype(jnp.bfloat16)
    window = lax.all_to_all(series, "node", split_axis=2, concat_axis=1, tiled=True)
    sent_rows = jnp.take(window, members, axis=1, mode="fill", fill_value=0)
    sent_rows = sent_rows.reshape(headings, owners, TILE_DEV, capacity, window_len)
    got_rows = lax.all_to_all(sent_rows, "freq", split_axis=1, concat_axis=1, tiled=True)
    got_weight = lax.all_to_all(sent_weight, "freq", split_axis=1, concat_axis=1, tiled=True)
    partial_value = jnp.einsum(
        "hskcw,skcn->hwkn", got_rows, got_weight[0], preferred_element_type=jnp.float32
    )
    node_loads = partial_value.reshape(partial_value.shape[0], partial_value.shape[1], -1)
    return node_loads.astype(jnp.bfloat16)


def solution(mesh):
    placed = (
        P(None, "freq", None, "node"),
        P(),
        P(),
        P("freq", None, None, None),
        P("freq", None, None, None),
    )
    return jax.shard_map(
        shards, mesh=mesh, in_specs=placed, out_specs=P(None, "node", "freq"), check_vma=False
    )
```

profile of v0, /device:TPU:1, one launch (start us, length us, event | category | flops | bytes accessed | tf_op | source)
XLA Modules:
  0.0 614.2 jit_solution(6448219081164938519)
XLA Ops:
  0.0 0.0 copy-start
  0.0 18.4 %copy.63 = bf16[2,4,4,8192]{2,1,0,3:T(4,128)(2,1)} copy(bf16[2,4,4,8192]{3,2,1,0:T(4,128)(2,1)} %param.5) | data formatting | bytes 1048576 | tf_op args[0]
  18.4 0.0 copy-start.3
  18.4 0.0 copy-start.4
  18.4 31.9 %reshape.201 = bf16[32,2,4096]{2,1,0:T(2,128)(2,1)} reshape(bf16[8192,2,4,4]{3,2,1,0:T(4,128)(2,1)} %bitcast.53) | data formatting | bytes 1048576
  50.2 8.6 %all-to-all-start.1 = ((bf16[32,2,4096]{2,1,0:T(2,128)(2,1)}), bf16[32,2,4096]{2,1,0:T(2,128)(2,1)S(1)}, u32[]{:S(2)}, u32[]{:S(2)}) async-start(bf16[32,2,4096]{2,1,0:T(2,128)(2,1)} %reshape.201), calls=%async_computation.1 | async-start | bytes 1048576 | tf_op jit(solution)/shard_map/all_to_all | solution.py:46
  58.8 0.0 copy-done.3
  58.9 0.1 copy.65
  59.0 0.1 copy.66
  59.1 0.0 copy-done.4
  59.1 0.1 copy.62
  59.2 9.0 %cosine_convert_fusion = (bf16[128,4096]{1,0:T(8,128)(2,1)S(1)}, bf16[128,4096]{1,0:T(8,128)(2,1)S(1)}) fusion(s32[128]{0:T(128)S(1)} %multiply_add_fusion), kind=kLoop, calls=%fused_computation.22 | loop fusion | flops 8912896 | bytes 2097664 | tf_op jit(solution)/shard_map/convert.2
  68.2 2.2 all-to-all-done.1
  70.4 37.1 %reshape.202 = bf16[8192,2,4,4]{3,2,1,0:T(4,128)(2,1)} reshape(bf16[32,2,4096]{2,1,0:T(2,128)(2,1)S(1)} %all-to-all-done.1) | data formatting | bytes 1048576
  107.6 22.6 %copy.64 = bf16[2,4,4,32,256]{4,2,1,3,0:T(4,128)(2,1)S(1)} copy(bf16[2,4,4,32,256]{2,1,0,4,3:T(4,128)(2,1)} %bitcast.52) | data formatting | bytes 1048576 | tf_op jit(solution)/shard_map/all_to_all | solution.py:46
  130.1 0.2 fusion.30
  130.3 0.5 fusion.21
  130.8 0.4 pad_maximum_fusion
  131.2 5.6 convolution_convert_fusion
  136.8 13.6 %copy.68 = bf16[4,256,4096]{1,0,2:T(4,128)(2,1)} copy(bf16[4,256,4096]{2,1,0:T(8,128)(2,1)} %convolution_convert_fusion) | data formatting | bytes 16777216 | tf_op jit(solution)/shard_map/convert_element_type | solution.py:67
  150.4 0.0 copy-start.2
  150.4 8.3 %all-to-all-start.2 = ((bf16[4,256,4096]{1,0,2:T(4,128)(2,1)}), bf16[4,256,4096]{1,0,2:T(4,128)(2,1)}, u32[]{:S(2)}, u32[]{:S(2)}) async-start(bf16[4,256,4096]{1,0,2:T(4,128)(2,1)} %copy.68), calls=%async_computation.2 | async-start | bytes 16777216 | tf_op jit(solution)/shard_map/all_to_all | solution.py:68
  158.8 0.0 copy-done.2
  158.8 0.1 copy.58
  158.9 0.3 fusion.14
  159.3 0.2 broadcast_add_fusion
  159.5 1.2 copy.59
  160.7 0.9 fusion.11
  161.7 8.1 %scatter_custom_fusion = s32[3072]{0:T(1024)S(1)} fusion(s32[2048]{0:T(1024)S(1)} %bitcast.67, s32[2048]{0:T(1024)S(1)} %iota.22, s32[]{:T(128)} %constant.33.clone.1), kind=kCustom, calls=%fused_computation.51 | custom fusion | bytes 12292 | tf_op jit(solution)/shard_map/scatter | solution.py:42
  169.8 0.2 broadcast_in_dim.35
  170.0 0.0 copy-done
  170.0 9.2 %gather_fusion = bf16[3072,128]{1,0:T(8,128)(2,1)S(1)} fusion(bf16[2048,128]{1,0:T(8,128)(2,1)S(1)} %bitcast.51, s32[3072]{0:T(1024)S(1)} %fusion.26), kind=kCustom, calls=%fused_computation | custom fusion | bytes 1585152 | tf_op jit(solution)/shard_map/jit(_take)/gather | solution.py:59
  179.2 0.2 gather.13
  179.4 0.7 broadcast_select_fusion.1
  180.1 1.1 copy.60
  181.2 164.8 %all-to-all-done.2 = bf16[4,256,4096]{1,0,2:T(4,128)(2,1)} async-done(((bf16[4,256,4096]{1,0,2:T(4,128)(2,1)}), bf16[4,256,4096]{1,0,2:T(4,128)(2,1)}, u32[]{:S(2)}, u32[]{:S(2)}) %all-to-all-start.2) | async-done | bytes 8388640 | tf_op jit(solution)/shard_map/all_to_all | solution.py:68
  345.9 5.2 all-to-all-start
  351.2 7.7 %copy.69 = bf16[4,256,4096]{1,2,0:T(8,128)(2,1)} copy(bf16[4,256,4096]{1,0,2:T(4,128)(2,1)} %all-to-all-done.2) | data formatting | bytes 16777216 | tf_op jit(solution)/shard_map/all_to_all | solution.py:68
  358.9 11.4 %copy.70 = bf16[4,8,256,512]{3,2,1,0:T(8,128)(2,1)} copy(bf16[4,8,256,512]{2,3,1,0:T(8,128)(2,1)} %bitcast.55) | data formatting | bytes 16777216 | tf_op jit(solution)/shard_map/all_to_all | solution.py:68
  370.2 12.1 %copy.71 = bf16[4,2048,512]{2,0,1:T(4,128)(2,1)} copy(bf16[4,2048,512]{2,1,0:T(8,128)(2,1)} %bitcast.56) | data formatting | bytes 16777216 | tf_op jit(solution)/shard_map/all_to_all | solution.py:68
  382.4 34.7 %gather_fusion.1 = bf16[3072,4,512]{2,1,0:T(4,128)(2,1)} fusion(bf16[4,2048,512]{2,0,1:T(4,128)(2,1)} %copy.71, s32[3072]{0:T(1024)S(1)} %fusion.26), kind=kCustom, calls=%fused_computation.1 | custom fusion | bytes 25178112 | tf_op jit(solution)/shard_map/jit(_take)/gather | solution.py:69
  417.1 9.1 %broadcast_select_fusion = bf16[4,32,8,12,512]{4,0,3,2,1:T(4,128)(2,1)S(1)} fusion(bf16[4,32,8,12,512]{4,0,3,2,1:T(4,128)(2,1)} %bitcast.54, pred[32,8,12]{2,1,0:T(8,128)(4,1)S(1)} %broadcast_in_dim.35), kind=kLoop, calls=%fused_computation.5 | loop fusion | flops 6291456 | bytes 25168896 | tf_op jit(solution)/shard_map/jit(_take)/select_n | solution.py:69
  426.2 11.4 %copy.72 = bf16[4,32,8,12,512]{4,2,3,0,1:T(8,128)(2,1)} copy(bf16[4,32,8,12,512]{4,0,3,2,1:T(4,128)(2,1)S(1)} %broadcast_select_fusion) | data formatting | bytes 25165824 | tf_op jit(solution)/shard_map/jit(_take)/select_n | solution.py:69
  437.7 0.0 all-to-all-done
  437.7 147.9 %all_to_all.43 = bf16[4,32,8,12,512]{4,2,3,0,1:T(8,128)(2,1)S(1)} all-to-all(bf16[4,32,8,12,512]{4,2,3,0,1:T(8,128)(2,1)} %copy.72), channel_id=1, replica_groups=mesh['freq'=32,'node'=8] {'freq'}, dimensions={1} | all-to-all | bytes 25165824 | tf_op jit(solution)/shard_map/all_to_all | solution.py:71
  585.6 17.9 %fusion.2 = bf16[4,512,8,128]{1,3,0,2:T(8,128)(2,1)} fusion(bf16[4,32,8,12,512]{4,2,3,0,1:T(8,128)(2,1)S(1)} %all_to_all.43, bf16[32,8,12,128,1]{3,1,2,0,4:T(8,128)(2,1)S(1)} %bitcast.62), kind=kOutput, calls=%fused_computation.8 | convolution fusion | flops 1612709888 | bytes 17563648 | tf_op jit(solution)/shard_map/hskcw,skcn->hwkn/dot_general | solution.py:73
  603.4 4.6 copy.74
  608.0 0.0 copy-start.1
  608.0 6.2 %copy.75 = bf16[4,512,1024]{2,1,0:T(8,128)(2,1)} copy(bf16[4,512,1024]{1,2,0:T(8,128)(2,1)} %bitcast.57) | data formatting | bytes 8388608 | tf_op jit(solution)/shard_map/convert_element_type | solution.py:77
  614.2 0.0 copy-done.1
  (10 shorter events, 0.1 us)
Async XLA Ops:
  0.0 170.0 %copy-start = (bf16[1,8,256,128]{3,2,1,0:T(8,128)(2,1)S(1)}, bf16[1,8,256,128]{3,2,1,0:T(8,128)(2,1)}, u32[]{:S(2)}) copy-start(bf16[1,8,256,128]{3,2,1,0:T(8,128)(2,1)} %param.9) | copy-start | bytes 1572868
  18.4 40.5 %copy-start.3 = (s32[4,128]{1,0:T(4,128)S(1)}, s32[4,128]{1,0:T(4,128)}, u32[]{:S(2)}) copy-start(s32[4,128]{1,0:T(4,128)} %param.7) | copy-start | bytes 6148
  18.4 40.7 %copy-start.4 = (f32[4,128]{1,0:T(4,128)S(1)}, f32[4,128]{1,0:T(4,128)}, u32[]{:S(2)}) copy-start(f32[4,128]{1,0:T(4,128)} %param.6) | copy-start | bytes 6148
  50.2 20.2 %all-to-all-start.1 = ((bf16[32,2,4096]{2,1,0:T(2,128)(2,1)}), bf16[32,2,4096]{2,1,0:T(2,128)(2,1)S(1)}, u32[]{:S(2)}, u32[]{:S(2)}) async-start(bf16[32,2,4096]{2,1,0:T(2,128)(2,1)} %reshape.201), calls=%async_computation.1 | async-start | bytes 1048576 | tf_op jit(solution)/shard_map/all_to_all | solution.py:46
  150.4 8.3 %copy-start.2 = (s32[1,8,256,1]{2,3,1,0:T(1,128)S(1)}, s32[1,8,256,1]{2,3,1,0:T(1,128)}, u32[]{:S(2)}) copy-start(s32[1,8,256,1]{2,3,1,0:T(1,128)} %param.8) | copy-start | bytes 24580
  150.4 195.5 %all-to-all-start.2 = ((bf16[4,256,4096]{1,0,2:T(4,128)(2,1)}), bf16[4,256,4096]{1,0,2:T(4,128)(2,1)}, u32[]{:S(2)}, u32[]{:S(2)}) async-start(bf16[4,256,4096]{1,0,2:T(4,128)(2,1)} %copy.68), calls=%async_computation.2 | async-start | bytes 16777216 | tf_op jit(solution)/shard_map/all_to_all | solution.py:68
  345.9 91.7 %all-to-all-start = ((bf16[1,32,8,12,128]{4,2,3,0,1:T(8,128)(2,1)}), bf16[1,32,8,12,128]{4,2,3,0,1:T(8,128)(2,1)S(1)}, u32[]{:S(2)}, u32[]{:S(2)}) async-start(bf16[1,32,8,12,128]{4,2,3,0,1:T(8,128)(2,1)} %copy.60), calls=%async_computation | async-start | bytes 1572864 | tf_op jit(solution)/shard_map/all_to_all | solution.py:72
  608.0 6.3 %copy-start.1 = (bf16[1,8,256,128]{3,2,1,0:T(8,128)(2,1)S(1)}, bf16[1,8,256,128]{3,2,1,0:T(8,128)(2,1)}, u32[]{:S(2)}) copy-start(bf16[1,8,256,128]{3,2,1,0:T(8,128)(2,1)} %param.9) | copy-start | bytes 1572868
where the time goes:
time: 618 us; the launch traced here: 614 us
  local copies, waits for them, and re-layouts  232 us (38%)
  waiting for transfers between devices  167 us (27%)
  blocking collectives  148 us (24%)
  matrix products  23.5 us (4%)
  starting transfers between devices  22.1 us (4%)
  other arithmetic  21.3 us (3%)
    all_to_all x1, waiting for transfers between devices, shards(): lax.all_to_all(series, 'node', split_axis=2, concat_axis=1, tiled=True)  165 us
    all_to_all x1, blocking collectives, shards(): lax.all_to_all(sent_rows, 'freq', split_axis=1, concat_axis=1, tiled=True)  148 us
    unnamed x13, local copies, waits for them, and re-layouts  87.4 us
    gather x1, local copies, waits for them, and re-layouts, shards(): sent_rows = jnp.take(window, members, axis=1, mode='fill', fill_value=0)  34.7 us
    all_to_all x3, local copies, waits for them, and re-layouts, shards(): lax.all_to_all(series, 'node', split_axis=2, concat_axis=1, tiled=True)  31.2 us
    all_to_all x1, local copies, waits for them, and re-layouts, shards(): lax.all_to_all(pressure, 'freq', split_axis=3, concat_axis=1, tiled=True)  22.6 us
    dot_general x1, matrix products, shards(): jnp.einsum('hskcw,skcn->hwkn', got_rows, got_weight[0], preferred_element...  17.9 us
    convert_element_type x1, local copies, waits for them, and re-layouts, shards(): series = jnp.einsum('khp,kt->hpt', scaled.reshape(2 * freq_count, heading...  13.6 us
  transfers between devices with their start and end apart: 3, of which 2 were waited for; matrix products, arithmetic and copies ran while one was open for 19% of the time, Pallas kernels for 0%

commit v1 on v0

--- a/solution.py
+++ b/solution.py
@@ -9,6 +9,12 @@
 BIN_STEP = 15
 PHASE_LEVELS = 4096
 TILE_DEV = 8
+
+
+def trade_parts(value, axis, split, join):
+    pieces = jnp.split(value, lax.axis_size(axis), axis=split)
+    got = lax.all_to_all(jnp.stack(pieces), axis, 0, 0)
+    return jnp.concatenate(got, axis=join)
 
 
 def scale_spectra(pressure, spectrum_amp, phase_code):
@@ -43,7 +49,7 @@
 
 
 def shards(pressure, spectrum_amp, phase_code, panel_tile, patch_weight):
-    regrouped = lax.all_to_all(pressure, "freq", split_axis=3, concat_axis=1, tiled=True)
+    regrouped = trade_parts(pressure, "freq", 3, 1)
     scaled = scale_spectra(regrouped, spectrum_amp, phase_code)
     freq_count = scaled.shape[1]
     headings = scaled.shape[2]

time: 618 us -> 549 us (0.89)
  local copies, waits for them, and re-layouts: 232 us -> 165 us
    unnamed x13 -> x41, local copies, waits for them, and re-layouts: 87.4 us -> 41.3 us
    all_to_all x1 -> x0, local copies, waits for them, and re-layouts: 22.6 us -> none  [shards(): lax.all_to_all(pressure, 'freq', split_axis=3, concat_axis=1, tiled=True)]
  transfers between devices with their start and end apart: 3 -> 3, of which waited for: 2 -> 2; matrix products, arithmetic and copies ran while one was open for 19% -> 22% of each run, Pallas kernels for 0% -> 0%
where the time goes in v1:
time: 549 us; the launch traced here: 546 us
  waiting for transfers between devices  167 us (30%)
  local copies, waits for them, and re-layouts  165 us (30%)
  blocking collectives  148 us (27%)
  matrix products  23.5 us (4%)
  starting transfers between devices  21.8 us (4%)
  other arithmetic  20.9 us (4%)
    all_to_all x1, waiting for transfers between devices, shards(): lax.all_to_all(series, 'node', split_axis=2, concat_axis=1, tiled=True)  165 us
    all_to_all x1, blocking collectives, shards(): lax.all_to_all(sent_rows, 'freq', split_axis=1, concat_axis=1, tiled=True)  148 us
    unnamed x41, local copies, waits for them, and re-layouts  41.3 us
    gather x1, local copies, waits for them, and re-layouts, shards(): sent_rows = jnp.take(window, members, axis=1, mode='fill', fill_value=0)  34.7 us
    all_to_all x3, local copies, waits for them, and re-layouts, shards(): lax.all_to_all(series, 'node', split_axis=2, concat_axis=1, tiled=True)  31.2 us
    dot_general x1, matrix products, shards(): jnp.einsum('hskcw,skcn->hwkn', got_rows, got_weight[0], preferred_element...  17.9 us
    convert_element_type x1, local copies, waits for them, and re-layouts, shards(): series = jnp.einsum('khp,kt->hpt', scaled.reshape(2 * freq_count, heading...  13.6 us
    select_n x1, local copies, waits for them, and re-layouts, shards(): sent_rows = jnp.take(window, members, axis=1, mode='fill', fill_value=0)  11.4 us
  transfers between devices with their start and end apart: 3, of which 2 were waited for; matrix products, arithmetic and copies ran while one was open for 22% of the time, Pallas kernels for 0%

profile of v1, /device:TPU:1, one launch (start us, length us, event | category | flops | bytes accessed | tf_op | source)
XLA Modules:
  0.0 546.2 jit_solution(18132354330567505870)
XLA Ops:
  0.0 1.4 constant_dynamic-update-slice_fusion.31
  1.4 1.3 constant_dynamic-update-slice_fusion.30
  2.7 1.3 constant_dynamic-update-slice_fusion.29
  4.1 1.3 constant_dynamic-update-slice_fusion.28
  5.4 1.3 constant_dynamic-update-slice_fusion.27
  6.7 1.3 constant_dynamic-update-slice_fusion.26
  8.1 1.3 constant_dynamic-update-slice_fusion.25
  9.4 1.3 constant_dynamic-update-slice_fusion.24
  10.7 1.3 constant_dynamic-update-slice_fusion.23
  12.0 1.3 constant_dynamic-update-slice_fusion.22
  13.4 1.3 constant_dynamic-update-slice_fusion.21
  14.7 1.3 constant_dynamic-update-slice_fusion.20
  16.0 1.3 constant_dynamic-update-slice_fusion.19
  17.4 1.3 constant_dynamic-update-slice_fusion.18
  18.7 1.3 constant_dynamic-update-slice_fusion.17
  20.0 1.3 constant_dynamic-update-slice_fusion.16
  21.3 1.3 constant_dynamic-update-slice_fusion.15
  22.7 1.3 constant_dynamic-update-slice_fusion.14
  24.0 1.3 constant_dynamic-update-slice_fusion.13
  25.3 1.3 constant_dynamic-update-slice_fusion.12
  26.7 1.3 constant_dynamic-update-slice_fusion.11
  28.0 1.3 constant_dynamic-update-slice_fusion.10
  29.3 1.3 constant_dynamic-update-slice_fusion.9
  30.6 1.3 constant_dynamic-update-slice_fusion.8
  32.0 1.3 constant_dynamic-update-slice_fusion.7
  33.3 1.3 constant_dynamic-update-slice_fusion.6
  34.6 1.3 constant_dynamic-update-slice_fusion.5
  36.0 1.3 constant_dynamic-update-slice_fusion.4
  37.3 1.3 constant_dynamic-update-slice_fusion.3
  38.6 1.3 constant_dynamic-update-slice_fusion.2
  39.9 1.3 constant_dynamic-update-slice_fusion.1
  41.3 1.3 constant_dynamic-update-slice_fusion
  42.6 8.6 %all-to-all-start.1 = ((bf16[32,2,4,4,256]{4,3,2,1,0:T(4,128)(2,1)}), bf16[32,2,4,4,256]{4,3,2,1,0:T(4,128)(2,1)S(1)}, u32[]{:S(2)}, u32[]{:S(2)}) async-start(bf16[32,2,4,4,256]{4,3,2,1,0:T(4,128)(2,1)} %constant_dynamic-update-slice_fusion), calls=%async_computation.1 | async-start | bytes 1048576 | tf_op jit(solution)/shard_map/all_to_all | solution.py:16
  51.2 9.0 %cosine_convert_fusion = (bf16[128,4096]{1,0:T(8,128)(2,1)S(1)}, bf16[128,4096]{1,0:T(8,128)(2,1)S(1)}) fusion(s32[128]{0:T(128)S(1)} %multiply_add_fusion), kind=kLoop, calls=%fused_computation.22 | loop fusion | flops 8912896 | bytes 2097664 | tf_op jit(solution)/shard_map/convert.2
  60.3 2.5 all-to-all-done.1
  62.8 0.2 fusion.23
  63.0 0.1 convert.18
  63.1 0.3 multiply_convert_fusion.1
  63.5 5.6 %convolution_convert_fusion = bf16[4,256,4096]{2,1,0:T(8,128)(2,1)} fusion(bf16[256,4,256]{2,0,1:T(8,128)(2,1)S(1)} %bitcast.119, bf16[128,4096]{1,0:T(8,128)(2,1)S(1)} %get-tuple-element.12, bf16[128,4096]{1,0:T(8,128)(2,1)S(1)} %get-tuple-element.11), kind=kOutput, calls=%fused_computation.7 | convolution fusion | flops 2155872256 | bytes 11010048 | tf_op jit(solution)/shard_map/khp,kt->hpt/dot_general | solution.py:68
  69.1 13.6 %copy.93 = bf16[4,256,4096]{1,0,2:T(4,128)(2,1)} copy(bf16[4,256,4096]{2,1,0:T(8,128)(2,1)} %convolution_convert_fusion) | data formatting | bytes 16777216 | tf_op jit(solution)/shard_map/convert_element_type | solution.py:73
  82.7 8.3 %all-to-all-start.2 = ((bf16[4,256,4096]{1,0,2:T(4,128)(2,1)}), bf16[4,256,4096]{1,0,2:T(4,128)(2,1)}, u32[]{:S(2)}, u32[]{:S(2)}) async-start(bf16[4,256,4096]{1,0,2:T(4,128)(2,1)} %copy.93), calls=%async_computation.2 | async-start | bytes 16777216 | tf_op jit(solution)/shard_map/all_to_all | solution.py:74
  91.1 0.1 copy.85
  91.2 0.3 fusion.14
  91.6 0.2 broadcast_add_fusion
  91.8 1.2 copy.86
  93.0 0.9 fusion.11
  94.0 8.1 %scatter_custom_fusion = s32[3072]{0:T(1024)S(1)} fusion(s32[2048]{0:T(1024)S(1)} %bitcast.127, s32[2048]{0:T(1024)S(1)} %iota.22, s32[]{:T(128)} %constant.33.clone.1), kind=kCustom, calls=%fused_computation.74 | custom fusion | bytes 12292 | tf_op jit(solution)/shard_map/scatter | solution.py:48
  102.1 0.2 broadcast_in_dim.35
  102.3 9.2 %gather_fusion = bf16[3072,128]{1,0:T(8,128)(2,1)S(1)} fusion(bf16[2048,128]{1,0:T(8,128)(2,1)S(1)} %bitcast.113, s32[3072]{0:T(1024)S(1)} %fusion.19), kind=kCustom, calls=%fused_computation | custom fusion | bytes 1585152 | tf_op jit(solution)/shard_map/jit(_take)/gather | solution.py:65
  111.5 0.2 gather.13
  111.6 0.7 broadcast_select_fusion.1
  112.4 1.1 copy.87
  113.5 164.8 %all-to-all-done.2 = bf16[4,256,4096]{1,0,2:T(4,128)(2,1)} async-done(((bf16[4,256,4096]{1,0,2:T(4,128)(2,1)}), bf16[4,256,4096]{1,0,2:T(4,128)(2,1)}, u32[]{:S(2)}, u32[]{:S(2)}) %all-to-all-start.2) | async-done | bytes 8388640 | tf_op jit(solution)/shard_map/all_to_all | solution.py:74
  278.2 4.9 all-to-all-start
  283.1 7.7 %copy.94 = bf16[4,256,4096]{1,2,0:T(8,128)(2,1)} copy(bf16[4,256,4096]{1,0,2:T(4,128)(2,1)} %all-to-all-done.2) | data formatting | bytes 16777216 | tf_op jit(solution)/shard_map/all_to_all | solution.py:74
  290.8 11.4 %copy.95 = bf16[4,8,256,512]{3,2,1,0:T(8,128)(2,1)} copy(bf16[4,8,256,512]{2,3,1,0:T(8,128)(2,1)} %bitcast.115) | data formatting | bytes 16777216 | tf_op jit(solution)/shard_map/all_to_all | solution.py:74
  302.2 12.1 %copy.96 = bf16[4,2048,512]{2,0,1:T(4,128)(2,1)} copy(bf16[4,2048,512]{2,1,0:T(8,128)(2,1)} %bitcast.116) | data formatting | bytes 16777216 | tf_op jit(solution)/shard_map/all_to_all | solution.py:74
  314.3 34.7 %gather_fusion.1 = bf16[3072,4,512]{2,1,0:T(4,128)(2,1)} fusion(bf16[4,2048,512]{2,0,1:T(4,128)(2,1)} %copy.96, s32[3072]{0:T(1024)S(1)} %fusion.19), kind=kCustom, calls=%fused_computation.1 | custom fusion | bytes 25178112 | tf_op jit(solution)/shard_map/jit(_take)/gather | solution.py:75
  349.1 9.1 %broadcast_select_fusion = bf16[4,32,8,12,512]{4,0,3,2,1:T(4,128)(2,1)S(1)} fusion(bf16[4,32,8,12,512]{4,0,3,2,1:T(4,128)(2,1)} %bitcast.114, pred[32,8,12]{2,1,0:T(8,128)(4,1)S(1)} %broadcast_in_dim.35), kind=kLoop, calls=%fused_computation.5 | loop fusion | flops 6291456 | bytes 25168896 | tf_op jit(solution)/shard_map/jit(_take)/select_n | solution.py:75
  358.2 11.4 %copy.97 = bf16[4,32,8,12,512]{4,2,3,0,1:T(8,128)(2,1)} copy(bf16[4,32,8,12,512]{4,0,3,2,1:T(4,128)(2,1)S(1)} %broadcast_select_fusion) | data formatting | bytes 25165824 | tf_op jit(solution)/shard_map/jit(_take)/select_n | solution.py:75
  369.6 147.9 %all_to_all.33 = bf16[4,32,8,12,512]{4,2,3,0,1:T(8,128)(2,1)S(1)} all-to-all(bf16[4,32,8,12,512]{4,2,3,0,1:T(8,128)(2,1)} %copy.97), channel_id=1, replica_groups=mesh['freq'=32,'node'=8] {'freq'}, dimensions={1} | all-to-all | bytes 25165824 | tf_op jit(solution)/shard_map/all_to_all | solution.py:77
  517.5 17.9 %fusion.2 = bf16[4,512,8,128]{1,3,0,2:T(8,128)(2,1)} fusion(bf16[4,32,8,12,512]{4,2,3,0,1:T(8,128)(2,1)S(1)} %all_to_all.33, bf16[32,8,12,128,1]{3,1,2,0,4:T(8,128)(2,1)S(1)} %bitcast.122), kind=kOutput, calls=%fused_computation.8 | convolution fusion | flops 1612709888 | bytes 17563648 | tf_op jit(solution)/shard_map/hskcw,skcn->hwkn/dot_general | solution.py:79
  535.4 4.6 copy.99
  539.9 6.2 %copy.100 = bf16[4,512,1024]{2,1,0:T(8,128)(2,1)} copy(bf16[4,512,1024]{1,2,0:T(8,128)(2,1)} %bitcast.117) | data formatting | bytes 8388608 | tf_op jit(solution)/shard_map/convert_element_type | solution.py:83
  (24 shorter events, 0.3 us)
Async XLA Ops:
  0.0 102.3 %copy-start = (bf16[1,8,256,128]{3,2,1,0:T(8,128)(2,1)S(1)}, bf16[1,8,256,128]{3,2,1,0:T(8,128)(2,1)}, u32[]{:S(2)}) copy-start(bf16[1,8,256,128]{3,2,1,0:T(8,128)(2,1)} %param.9) | copy-start | bytes 1572868
  0.0 60.2 %copy-start.4 = (s32[4,128]{1,0:T(4,128)S(1)}, s32[4,128]{1,0:T(4,128)}, u32[]{:S(2)}) copy-start(s32[4,128]{1,0:T(4,128)} %param.7) | copy-start | bytes 6148
  42.6 20.2 %all-to-all-start.1 = ((bf16[32,2,4,4,256]{4,3,2,1,0:T(4,128)(2,1)}), bf16[32,2,4,4,256]{4,3,2,1,0:T(4,128)(2,1)S(1)}, u32[]{:S(2)}, u32[]{:S(2)}) async-start(bf16[32,2,4,4,256]{4,3,2,1,0:T(4,128)(2,1)} %constant_dynamic-update-slice_fusion), calls=%async_computation.1 | async-start | bytes 1048576 | tf_op jit(solution)/shard_map/all_to_all | solution.py:16
  51.2 11.9 %copy-start.3 = (f32[4,128]{1,0:T(4,128)S(1)}, f32[4,128]{1,0:T(4,128)}, u32[]{:S(2)}) copy-start(f32[4,128]{1,0:T(4,128)} %param.6) | copy-start | bytes 6148
  82.7 8.3 %copy-start.2 = (s32[1,8,256,1]{2,3,1,0:T(1,128)S(1)}, s32[1,8,256,1]{2,3,1,0:T(1,128)}, u32[]{:S(2)}) copy-start(s32[1,8,256,1]{2,3,1,0:T(1,128)} %param.8) | copy-start | bytes 24580
  82.7 195.5 %all-to-all-start.2 = ((bf16[4,256,4096]{1,0,2:T(4,128)(2,1)}), bf16[4,256,4096]{1,0,2:T(4,128)(2,1)}, u32[]{:S(2)}, u32[]{:S(2)}) async-start(bf16[4,256,4096]{1,0,2:T(4,128)(2,1)} %copy.93), calls=%async_computation.2 | async-start | bytes 16777216 | tf_op jit(solution)/shard_map/all_to_all | solution.py:74
  278.2 91.4 %all-to-all-start = ((bf16[1,32,8,12,128]{4,2,3,0,1:T(8,128)(2,1)}), bf16[1,32,8,12,128]{4,2,3,0,1:T(8,128)(2,1)S(1)}, u32[]{:S(2)}, u32[]{:S(2)}) async-start(bf16[1,32,8,12,128]{4,2,3,0,1:T(8,128)(2,1)} %copy.87), calls=%async_computation | async-start | bytes 1572864 | tf_op jit(solution)/shard_map/all_to_all | solution.py:78
  539.9 6.3 %copy-start.1 = (bf16[1,8,256,128]{3,2,1,0:T(8,128)(2,1)S(1)}, bf16[1,8,256,128]{3,2,1,0:T(8,128)(2,1)}, u32[]{:S(2)}) copy-start(bf16[1,8,256,128]{3,2,1,0:T(8,128)(2,1)} %param.9) | copy-start | bytes 1572868
